TPU v7x, 512 devices: a whole 4x8x8 slice. The times are simulated.
512 devices in a mesh: cls: 64 (over x, z, y_hi), dp: 8 (over y_lo, core).
Axes of the slice: x: 4, y: 8 (y_hi: 2, y_lo: 4; y = y_hi * 4 + y_lo), z: 8, core: 2. Of those that a mesh axis runs over, the one named last changes fastest.
Arguments:
- features: bfloat16 [65536, 512], P(('cls', 'dp')), may hold values from -6 to 6
- labels: int32 [65536], P(('cls', 'dp')), may hold values from 0 to 16383, as said below
- weights: float32 [65536, 512], P('cls'), may hold values from -0.25 to 0.25
- sampled: int32 [16384], P('cls'), may hold values from 0 to 1023, as said below
Outputs:
- sample_loss: float32 [65536], P(('cls', 'dp'))
- weight_grad: float32 [16384, 512], P(('cls', 'dp'))
Inputs may be any that keep to these rules, and one draw needn't show every extreme that they name: The owner of a label is label // 256. In the rows of one device (aligned blocks of 128 rows) exactly one owner receives 4 of the labels and every other owner fewer. `sampled`: each aligned block of 256 entries holds distinct rows of the owner's bank.
All inputs are finite; a program needn't handle non-finite values.
Results may differ from a plain program's by a relative error of at most 0.0038.
Values may be sent and summed in bfloat16 or wider, within the bound.
A program may use at most 64 MiB of HBM per device.

v0:
```python
import math

import jax
import jax.numpy as jnp
from jax import lax
from jax.sharding import PartitionSpec as P

logit_scale = 64.0
margin = 0.35
epsilon = 1e-06


def normalize_rows(matrix):
    squares = jnp.sum(matrix * matrix, axis=1, keepdims=True)
    return lax.rsqrt(squares + epsilon)


def logits_of(feat_block, label_block, class_block, class_ids):
    cosine = jnp.dot(feat_block, class_block.T, preferred_element_type=jnp.float32)
    target_hit = label_block[:, None] == class_ids[None, :]
    logits = logit_scale * (cosine - margin * target_hit.astype(jnp.float32))
    return (logits, target_hit)


def per_device(features, labels, weights, sampled):
    groups = lax.axis_size("cls")
    replicas = lax.axis_size("dp")
    position = lax.axis_index("cls")
    local_rows = features.shape[0]
    feature_width = features.shape[1]
    classes = sampled.shape[0]
    capacity = local_rows // groups + 2
    feat_wide = features.astype(jnp.float32)
    unit_feats = (feat_wide * normalize_rows(feat_wide)).astype(jnp.bfloat16)
    chosen = weights[sampled]
    inverse_norm = normalize_rows(chosen)
    unit_f32 = chosen * inverse_norm
    unit_rows = unit_f32.astype(jnp.bfloat16)
    owner_ids = labels // classes
    column = labels % classes
    owner_hits = (owner_ids[:, None] == jnp.arange(groups, dtype=jnp.int32)[None, :]).astype(
        jnp.int32
    )
    earlier = jnp.cumsum(owner_hits, axis=0) - owner_hits
    ranking = jnp.sum(earlier * owner_hits, axis=1)
    buffer_slot = owner_ids * capacity + ranking
    slot_codes = jnp.arange(local_rows, dtype=jnp.int32) * classes + column
    outgoing = jnp.full((groups * capacity,), -1, jnp.int32).at[buffer_slot].set(slot_codes)
    outgoing = outgoing.reshape(groups, capacity)
    gathered = lax.all_gather(unit_feats, "cls", axis=0, tiled=True)
    group_rows = gathered.shape[0]

    def decode(incoming):
        is_valid = incoming >= 0
        safe_code = jnp.maximum(incoming, 0)
        source_row = (
            jnp.arange(incoming.shape[0], dtype=jnp.int32)[:, None] * local_rows
            + safe_code // classes
        )
        return (is_valid, source_row, safe_code % classes)

    incoming = lax.all_to_all(outgoing, "cls", split_axis=0, concat_axis=0, tiled=True)
    is_valid, source_row, class_col = decode(incoming)
    feat_rows = gathered[source_row].astype(jnp.float32)
    class_rows = unit_rows[class_col].astype(jnp.float32)
    cosine = jnp.sum(feat_rows * class_rows, axis=2)
    values = logit_scale * (cosine - margin)
    replies = lax.all_to_all(values, "cls", split_axis=0, concat_axis=0, tiled=True)
    replies, incoming = (replies, incoming)
    is_valid, source_row, class_col = decode(incoming)
    drop_index = jnp.where(is_valid, source_row, group_rows).reshape(-1)
    label_local = (
        jnp.full((group_rows,), -1, jnp.int32)
        .at[drop_index]
        .set(class_col.reshape(-1), mode="drop")
    )
    block_rows = math.gcd(group_rows, 512)
    count_blocks = group_rows // block_rows
    feat_blocks = gathered.reshape(count_blocks, block_rows, feature_width)
    label_blocks = label_local.reshape(count_blocks, block_rows)
    all_ids = jnp.arange(classes, dtype=jnp.int32)

    def first_pass(operands):
        logits, target_hit = logits_of(operands[0], operands[1], unit_rows, all_ids)
        part_sum = jnp.sum(jnp.exp(logits - logit_scale), axis=1)
        part_target = jnp.sum(jnp.where(target_hit, logits, 0.0), axis=1)
        return (part_sum, part_target)

    part_sum, part_target = lax.map(first_pass, (feat_blocks, label_blocks))
    part_sum = part_sum.reshape(group_rows)
    part_target = part_target.reshape(group_rows)
    own_start = position * local_rows
    totals = lax.psum(part_sum, "cls")
    own_target = replies.reshape(-1)[buffer_slot]
    own_total = lax.dynamic_slice_in_dim(totals, own_start, local_rows)
    sample_loss = logit_scale + jnp.log(own_total) - own_target
    total_blocks = totals.reshape(count_blocks, block_rows)
    class_ids = jnp.arange(lax.axis_size("dp") * (classes // replicas), dtype=jnp.int32)

    def accumulate(running, triple):
        logits, target_hit = logits_of(triple[0], triple[1], unit_rows, class_ids)
        softmax = jnp.exp(logits - logit_scale) / triple[2][:, None]
        grads_low = (logit_scale * (softmax - target_hit.astype(jnp.float32)) / replicas).astype(
            jnp.bfloat16
        )
        return (running + jnp.dot(grads_low.T, triple[0], preferred_element_type=jnp.float32), None)

    start_grad = jnp.zeros(
        (lax.axis_size("dp") * (classes // replicas), feature_width), jnp.float32
    )
    unit_grad, _ = lax.scan(accumulate, start_grad, (feat_blocks, label_blocks, total_blocks))
    radial = jnp.sum(unit_f32 * unit_grad, axis=1, keepdims=True)
    weight_grad = lax.psum_scatter(
        inverse_norm * (unit_grad - unit_f32 * radial), "dp", scatter_dimension=0, tiled=True
    )
    return (sample_loss, weight_grad)


def solution(mesh):
    in_specs = (P(("cls", "dp"), None), P(("cls", "dp")), P("cls", None), P("cls"))
    out_specs = (P(("cls", "dp")), P(("cls", "dp"), None))
    return jax.shard_map(
        per_device, mesh=mesh, in_specs=in_specs, out_specs=out_specs, check_vma=False
    )
```

profile of v0, /device:TPU:1, one launch (start us, length us, event | category | flops | bytes accessed | tf_op | source)
XLA Modules:
  0.0 771.1 jit_solution(14654492984104845493)
XLA Ops:
  8.4 1.7 fusion.41
  12.9 19.6 %all-to-all-start = ((s32[64,1,4]{2,1,0:T(1,128)}), s32[64,1,4]{2,1,0:T(1,128)S(1)}, u32[]{:S(2)}, u32[]{:S(2)}) async-start(s32[64,1,4]{2,1,0:T(1,128)} %bitcast.1), calls=%async_computation | async-start | bytes 65536 | tf_op jit(solution)/shard_map/all_to_all | solution.py:62
  35.1 10.5 %all-to-all-done = s32[64,1,4]{2,1,0:T(1,128)S(1)} async-done(((s32[64,1,4]{2,1,0:T(1,128)}), s32[64,1,4]{2,1,0:T(1,128)S(1)}, u32[]{:S(2)}, u32[]{:S(2)}) %all-to-all-start) | async-done | bytes 1056 | tf_op jit(solution)/shard_map/all_to_all | solution.py:62
  46.3 1.4 scatter_custom_fusion.1
  47.8 158.5 %all-gather.2.cloned.1.call-done = bf16[8192,512]{1,0:T(8,128)(2,1)} async-done(((bf16[128,512]{1,0:T(8,128)(2,1)}), bf16[8192,512]{1,0:T(8,128)(2,1)}) %all-gather.2.cloned.1.call-update) | async-done | bytes 8388624 | tf_op jit(solution)/shard_map/all_gather | solution.py:50
  206.2 44.7 %while.26 = (s32[]{:T(128)}, f32[16,512]{1,0:T(8,128)}, bf16[16,512,512]{2,1,0:T(8,128)(2,1)}, bf16[256,512]{1,0:T(8,128)(2,1)S(1)}, s32[16,512]{1,0:T(8,128)S(1)}, /*index=5*/s32[]{:T(128)}, s32[]{:T(128)}) while((s32[]{:T(128)}, f32[16,512]{1,0:T(8,128)}, bf16[16,512,512]{2,1,0:T(8,128)(2,1)}, bf16[256,512]{1,0:T(8,128)(2,1)S(1)}, ...), condition=%wide.region_8.9_spmd.clone, body=%wide.region_6.8_spmd.clone.sunk | while | flops 135003648 | bytes 798817 | solution.py:89
  211.8 1.4 fusion.63
  223.0 1.4 fusion.63
  234.2 1.4 fusion.63
  251.8 373.9 %psum.7 = f32[8192]{0:T(1024)S(1)} all-reduce(f32[8192]{0:T(1024)S(1)} %bitcast.77), channel_id=1, replica_groups=mesh['cls'=64,'dp'=8] {'cls'}, use_global_device_ids=true, to_apply=%region_9.10 | all-reduce | flops 8192 | bytes 65536 | tf_op jit(solution)/shard_map/psum | solution.py:93
  625.7 47.0 %while.27 = (s32[]{:T(128)}, f32[256,512]{1,0:T(8,128)S(1)}, bf16[16,512,512]{2,1,0:T(8,128)(2,1)}, bf16[256,512]{1,0:T(8,128)(2,1)S(1)}, s32[16,512]{1,0:T(8,12...) while((s32[]{:T(128)}, f32[256,512]{1,0:T(8,128)S(1)}, bf16[16,512,512]{2,1,0:T(8,128)(2,1)}, ...), condition=%wide.region_12.13_spmd.clone, body=%wide.region_11.12_spmd.clone.sunk | while | flops 270008320 | bytes 2373230 | solution.py:111
  626.5 2.1 convolution_add_fusion.2
  629.4 2.1 convolution_add_fusion.2
  632.3 2.1 convolution_add_fusion.2
  635.2 2.2 convolution_add_fusion.2
  638.2 2.1 convolution_add_fusion.2
  641.1 2.2 convolution_add_fusion.2
  644.0 2.1 convolution_add_fusion.2
  647.0 2.1 convolution_add_fusion.2
  649.9 2.1 convolution_add_fusion.2
  652.8 2.2 convolution_add_fusion.2
  655.7 2.1 convolution_add_fusion.2
  658.7 2.2 convolution_add_fusion.2
  661.6 2.2 convolution_add_fusion.2
  664.5 2.3 convolution_add_fusion.2
  667.6 2.2 convolution_add_fusion.2
  670.5 2.1 convolution_add_fusion.2
  673.6 1.7 subtract_multiply_fusion
  677.3 5.7 gather_fusion.1
  683.9 4.6 all-to-all-start.1
  688.5 13.1 %all-to-all-done.1 = f32[64,1,4]{2,1,0:T(1,128)S(1)} async-done(((f32[64,1,4]{2,1,0:T(1,128)}), f32[64,1,4]{2,1,0:T(1,128)S(1)}, u32[]{:S(2)}, u32[]{:S(2)}) %all-to-all-start.1) | async-done | bytes 1056 | tf_op jit(solution)/shard_map/all_to_all | solution.py:68
  704.8 59.4 %reduce-scatter.2.cloned.1.call-done = f32[32,512]{1,0:T(8,128)} async-done(((f32[256,512]{1,0:T(8,128)}), f32[32,512]{1,0:T(8,128)}) %reduce-scatter.2.cloned.1.call-update) | async-done | bytes 65552 | tf_op jit(solution)/shard_map/reduce_scatter | solution.py:113
  (144 shorter events, 67.2 us)
Async XLA Ops:
  7.2 26.1 %copy-start = (f32[1024,512]{1,0:T(8,128)S(1)}, f32[1024,512]{1,0:T(8,128)}, u32[]{:S(2)}) copy-start(f32[1024,512]{1,0:T(8,128)} %param.10) | copy-start | bytes 6291460
  7.2 199.1 %all-gather.2.cloned.1.call-start = ((), (), s32[]{:S(2)}) async-start(), calls=%async_computation.3 | async-start | bytes 8519680 | tf_op jit(solution)/shard_map/all_gather | solution.py:50
  11.2 21.3 %copy-start.4 = (s32[128]{0:T(128)}, s32[128]{0:T(128)S(1)}, u32[]{:S(2)}) copy-start(s32[128]{0:T(128)S(1)} %compare_select_fusion.4) | copy-start | bytes 1540
  12.9 32.7 %all-to-all-start = ((s32[64,1,4]{2,1,0:T(1,128)}), s32[64,1,4]{2,1,0:T(1,128)S(1)}, u32[]{:S(2)}, u32[]{:S(2)}) async-start(s32[64,1,4]{2,1,0:T(1,128)} %bitcast.1), calls=%async_computation | async-start | bytes 65536 | tf_op jit(solution)/shard_map/all_to_all | solution.py:62
  32.5 731.8 %reduce-scatter.2.cloned.1.call-start = ((), (), s32[]{:S(2)}) async-start(), calls=%async_computation.4 | async-start | bytes 589824 | tf_op jit(solution)/shard_map/reduce_scatter | solution.py:113
  34.4 0.6 copy-start.2
  34.5 11.3 %copy-start.3 = (s32[64]{0:T(128)}, s32[64]{0:T(128)S(1)}, u32[]{:S(2)}) copy-start(s32[64]{0:T(128)S(1)} %iota_multiply_fusion) | copy-start | bytes 772
  251.0 0.8 copy-start.1
  672.7 15.8 %copy-start.5 = (s32[128]{0:T(128)S(1)}, s32[128]{0:T(128)}, u32[]{:S(2)}) copy-start(s32[128]{0:T(128)} %copy-done.4) | copy-start | bytes 1540
  683.9 17.7 %all-to-all-start.1 = ((f32[64,1,4]{2,1,0:T(1,128)}), f32[64,1,4]{2,1,0:T(1,128)S(1)}, u32[]{:S(2)}, u32[]{:S(2)}) async-start(f32[64,1,4]{2,1,0:T(1,128)} %bitcast.10), calls=%async_computation.1 | async-start | bytes 65536 | tf_op jit(solution)/shard_map/all_to_all | solution.py:68
Sparse Core Ops, SparseCore 0:
  12.5 193.7 all-gather.1
  675.4 88.8 reduce-scatter.1
where the time goes:
time: 777 us; the launch traced here: 771 us
  blocking collectives  374 us (48%)
  waiting for transfers between devices  241 us (31%)
  matrix products  57.7 us (7%)
  local copies, waits for them, and re-layouts  49 us (6%)
  starting transfers between devices  24.3 us (3%)
  between operations  14.4 us (2%)
  other arithmetic  9.74 us (1%)
    psum x1, blocking collectives, per_device(): totals = lax.psum(part_sum, 'cls')  374 us
    all_gather x1, waiting for transfers between devices, per_device(): gathered = lax.all_gather(unit_feats, 'cls', axis=0, tiled=True)  158 us
    reduce_scatter x1, waiting for transfers between devices, per_device(): lax.psum_scatter(inverse_norm * (unit_grad - unit_f32 * radial), 'dp', sc...  59.4 us
    dot_general x16, matrix products, accumulate(): jnp.dot(grads_low.T, triple[0], preferred_element_type=jnp.float32)  34.6 us
    dot_general x16, matrix products, logits_of(): jnp.dot(feat_block, class_block.T, preferred_element_type=jnp.float32)  23 us
    dynamic_update_slice x16, local copies, waits for them, and re-layouts, per_device(): part_sum, part_target = lax.map(first_pass, (feat_blocks, label_blocks))  21.5 us
    all_to_all x1, starting transfers between devices, per_device(): lax.all_to_all(outgoing, 'cls', split_axis=0, concat_axis=0, tiled=True)  19.6 us
  transfers between devices with their start and end apart: 4, of which 4 were waited for; matrix products, arithmetic and copies ran while one was open for 2% of the time, Pallas kernels for 0%

commit v1 on v0

v1 whole, which is shorter than its diff:
```python
import functools

import jax
import jax.numpy as jnp
from jax import lax
from jax.experimental import pallas as pl
from jax.experimental.pallas import tpu as pltpu
from jax.sharding import PartitionSpec as P

logit_scale = 64.0
margin = 0.35
epsilon = 1e-06

NX, NZ, NYH, NYL, NCORE = 4, 8, 2, 4, 2
ROWS = 128
OUT_ROWS = 32
WIDTH = 512
PAIR = 2 * ROWS


def normalize_rows(matrix):
    squares = jnp.sum(matrix * matrix, axis=1, keepdims=True)
    return lax.rsqrt(squares + epsilon)


def head_kernel(
    feat_ref,
    label_ref,
    class_ref,
    unit_ref,
    inverse_ref,
    loss_ref,
    grad_ref,
    feats,
    classes,
    labels,
    ids,
    probs,
    grads,
    inverse_total,
    sums,
    sums_in,
    targets,
    targets_in,
    part_out,
    part_in,
    part_own,
    half_out,
    half_own,
    half_in,
    feat_send,
    feat_recv,
    core_send,
    core_recv,
    label_send,
    label_recv,
    class_send,
    class_recv,
    sum_send,
    sum_recv,
    target_send,
    target_recv,
    part_send,
    part_recv,
    half_send,
    half_recv,
):
    cls, dp = lax.axis_index("cls"), lax.axis_index("dp")
    x, z, yh = lax.div(cls, 16), lax.rem(lax.div(cls, 2), 8), lax.rem(cls, 2)
    yl, core = lax.div(dp, 2), lax.rem(dp, 2)

    def device(dx=0, dz=0, dyh=0, dyl=0, dcore=0):
        px = lax.rem(x + dx, NX)
        pz = lax.rem(z + dz, NZ)
        pyh = lax.rem(yh + dyh, NYH)
        pyl = lax.rem(yl + dyl, NYL)
        pcore = lax.rem(core + dcore, NCORE)
        return ((px * NZ + pz) * NYH + pyh, pyl * NCORE + pcore)

    mirror = ((x * NZ + z) * NYH + (1 - yh), (NYL - 1 - yl) * NCORE + core)

    def copy(src, dst, send, recv, target):
        return pltpu.make_async_remote_copy(
            src_ref=src,
            dst_ref=dst,
            send_sem=send,
            recv_sem=recv,
            device_id=target,
            device_id_type=pl.DeviceIdType.MESH,
        )

    plane = [(o, w) for o in range(NZ) for w in range(NCORE) if (o, w) != (0, 0)]
    column = [(u, v) for u in range(NYH) for v in range(NYL) if (u, v) != (0, 0)]

    barrier = pltpu.get_barrier_semaphore()
    peers = [device(dz=o, dcore=w) for o, w in plane]
    peers += [device(dx=i) for i in range(1, NX)]
    peers += [device(dyh=u, dyl=v) for u, v in column]
    for peer in peers:
        pl.semaphore_signal(barrier, inc=1, device_id=peer, device_id_type=pl.DeviceIdType.MESH)
    pl.semaphore_wait(barrier, len(peers))

    def feat_copy(slot):
        if slot <= NZ // 2:
            came, target = slot - 1, device(dz=1)
        else:
            came, target = (slot + 1) % NZ, device(dz=NZ - 1)
        src = feat_ref if came == 0 else feats.at[came, pl.ds(0, ROWS)]
        return copy(
            src, feats.at[slot, pl.ds(0, ROWS)], feat_send.at[slot], feat_recv.at[slot], target
        )

    def core_copy(slot):
        src = feat_ref if slot == 0 else feats.at[slot, pl.ds(0, ROWS)]
        return copy(
            src,
            feats.at[slot, pl.ds(ROWS, ROWS)],
            core_send.at[slot],
            core_recv.at[slot],
            device(dcore=1),
        )

    def class_copy(i, u):
        if i == 0:
            src, target = class_ref, mirror
        else:
            src = class_ref if u == 0 else classes.at[0, pl.ds(ROWS, ROWS)]
            target = device(dx=i)
        k = 2 * i + u
        return copy(
            src, classes.at[i, pl.ds(u * ROWS, ROWS)], class_send.at[k], class_recv.at[k], target
        )

    def label_copy(o, w):
        k = 2 * o + w
        return copy(
            label_ref, labels.at[k], label_send.at[k], label_recv.at[k], device(dz=o, dcore=w)
        )

    feat_copies = {s: feat_copy(s) for s in range(1, NZ)}
    core_copies = {s: core_copy(s) for s in range(NZ)}
    class_copies = {(i, u): class_copy(i, u) for i in range(NX) for u in range(2) if i + u}
    label_copies = [label_copy(o, w) for o, w in plane]

    class_copies[0, 1].start()
    feat_copies[1].start()
    feat_copies[NZ - 1].start()
    for i in (2, 1, 3):
        class_copies[i, 0].start()
    core_copies[0].start()
    for one in label_copies:
        one.start()

    feats[0, :ROWS] = feat_ref[...]
    classes[0, :ROWS] = class_ref[...]
    labels[0] = label_ref[...]
    row = lax.broadcasted_iota(jnp.int32, (PAIR, PAIR), 0)
    upper = row >= ROWS
    within = jnp.where(upper, row - ROWS, row)
    ids[...] = (
        z * (2 * PAIR)
        + jnp.where(upper, (1 - yh) * PAIR, yh * PAIR)
        + lax.shift_right_logical(within, 5) * (2 * OUT_ROWS)
        + core * OUT_ROWS
        + lax.bitwise_and(within, OUT_ROWS - 1)
    )

    for step in range(1, NZ // 2 + 1):
        feat_copies[step].wait_recv()
        if step < NZ // 2:
            feat_copies[step + 1].start()
        core_copies[step].start()
        if step < NZ // 2:
            feat_copies[NZ - step].wait_recv()
            if step < NZ // 2 - 1:
                feat_copies[NZ - step - 1].start()
            core_copies[NZ - step].start()
        if step == 1:
            class_copies[0, 1].wait_recv()
            for i in (2, 1, 3):
                class_copies[i, 1].start()

    for one in label_copies:
        one.wait_recv()
    for one in core_copies.values():
        one.wait_recv()
    for key, one in class_copies.items():
        if key != (0, 1):
            one.wait_recv()

    def hits(s, i):
        names = jnp.concatenate([labels[2 * s], labels[2 * s + 1]], axis=1)
        bank = lax.rem(x + (NX - i), NX) * (NZ * NYH * PAIR)
        return ids[...] == names - bank

    def first_pass(s, carry):
        block = feats[s]
        total = jnp.zeros((1, PAIR), jnp.float32)
        target = jnp.zeros((1, PAIR), jnp.float32)
        for i in range(NX):
            cosine = lax.dot_general(
                classes[i],
                block,
                (((1,), (1,)), ((), ())),
                preferred_element_type=jnp.float32,
            )
            hit = hits(s, i)
            logits = logit_scale * (cosine - jnp.where(hit, margin, 0.0))
            prob = jnp.exp(logits - logit_scale)
            probs[i, s] = prob
            total += jnp.sum(prob, axis=0, keepdims=True)
            target += jnp.sum(jnp.where(hit, logits, 0.0), axis=0, keepdims=True)
        sums[0, pl.ds(s, 1)] = total[:, :ROWS]
        sums[1, pl.ds(s, 1)] = total[:, ROWS:]
        targets[2 * s] = target[:, :ROWS]
        targets[2 * s + 1] = target[:, ROWS:]
        return carry

    lax.fori_loop(0, NZ, first_pass, 0)

    sum_copies, target_copies = {}, {}
    for o, w in plane:
        k = 2 * o + w
        sum_copies[o, w] = copy(
            sums, sums_in.at[k], sum_send.at[k], sum_recv.at[k], device(dz=o, dcore=w)
        )
        target_copies[o, w] = copy(
            targets.at[k],
            targets_in.at[k],
            target_send.at[k],
            target_recv.at[k],
            device(dz=NZ - o, dcore=w),
        )
    for one in sum_copies.values():
        one.start()
    for one in target_copies.values():
        one.start()
    whole = [sums[0], sums[1]]
    for (o, w), one in sum_copies.items():
        one.wait_recv()
        for q in range(2):
            other = sums_in[2 * o + w, (q + w) % 2]
            whole[q] += other if o == 0 else pltpu.roll(other, o, 0)
    for q in range(2):
        inverse_total[q] = 1.0 / whole[q]

    part_copies = {}
    for i in (2, 1, 3, 0):

        def weigh(s, carry):
            inverse = jnp.concatenate(
                [inverse_total[0, pl.ds(s, 1)], inverse_total[1, pl.ds(s, 1)]], axis=1
            )
            hit = hits(s, i)
            slope = (logit_scale / 8.0) * (probs[i, s] * inverse - jnp.where(hit, 1.0, 0.0))
            grads[s] = slope.astype(jnp.bfloat16)
            return carry

        lax.fori_loop(0, NZ, weigh, 0)
        part = jnp.zeros((PAIR, WIDTH), jnp.float32)
        for s in range(NZ):
            part += jnp.dot(grads[s], feats[s], preferred_element_type=jnp.float32)
        if i == 0:
            part_own[...] = part
        else:
            part_out[i] = part.astype(jnp.bfloat16)
            part_copies[i] = copy(
                part_out.at[i],
                part_in.at[i],
                part_send.at[i],
                part_recv.at[i],
                device(dx=NX - i),
            )
            part_copies[i].start()

    own_target = targets[0]
    for (o, w), one in target_copies.items():
        one.wait_recv()
        own_target += targets_in[2 * o + w]
    loss_ref[...] = logit_scale + jnp.log(whole[0][0:1]) - own_target

    half = part_own[...]
    for i in (1, 3, 2):
        part_copies[i].wait_recv()
        half += part_in[i].astype(jnp.float32)
    half = half.reshape(NYH * NYL, OUT_ROWS, WIDTH)
    half_own[...] = half
    half_out[...] = half.astype(jnp.bfloat16)
    half_copies = {}
    for u, v in column:
        k = NYL * u + v
        half_copies[u, v] = copy(
            half_out.at[NYL * u + lax.rem(yl + v, NYL)],
            half_in.at[k],
            half_send.at[k],
            half_recv.at[k],
            device(dyh=u, dyl=v),
        )
        half_copies[u, v].start()
    total = half_own[yl]
    for (u, v), one in half_copies.items():
        one.wait_recv()
        total += half_in[NYL * u + v].astype(jnp.float32)
    unit = unit_ref[...]
    radial = jnp.sum(unit * total, axis=1, keepdims=True)
    grad_ref[...] = inverse_ref[...] * (total - unit * radial)

    for group in (
        feat_copies,
        core_copies,
        class_copies,
        sum_copies,
        target_copies,
        part_copies,
        half_copies,
    ):
        for one in group.values():
            one.wait_send()
    for one in label_copies:
        one.wait_send()


def head(unit_feats, labels, class_rows, unit_own, inverse_own):
    vmem = pl.BlockSpec(memory_space=pltpu.VMEM)
    dma = pltpu.SemaphoreType.DMA
    slots = NZ * NCORE
    scratch = [
        pltpu.VMEM((NZ, PAIR, WIDTH), jnp.bfloat16),
        pltpu.VMEM((NX, PAIR, WIDTH), jnp.bfloat16),
        pltpu.VMEM((slots, 1, ROWS), jnp.int32),
        pltpu.VMEM((PAIR, PAIR), jnp.int32),
        pltpu.VMEM((NX, NZ, PAIR, PAIR), jnp.float32),
        pltpu.VMEM((NZ, PAIR, PAIR), jnp.bfloat16),
        pltpu.VMEM((2, NZ, ROWS), jnp.float32),
        pltpu.VMEM((2, NZ, ROWS), jnp.float32),
        pltpu.VMEM((slots, 2, NZ, ROWS), jnp.float32),
        pltpu.VMEM((slots, 1, ROWS), jnp.float32),
        pltpu.VMEM((slots, 1, ROWS), jnp.float32),
        pltpu.VMEM((NX, PAIR, WIDTH), jnp.bfloat16),
        pltpu.VMEM((NX, PAIR, WIDTH), jnp.bfloat16),
        pltpu.VMEM((PAIR, WIDTH), jnp.float32),
        pltpu.VMEM((NYH * NYL, OUT_ROWS, WIDTH), jnp.bfloat16),
        pltpu.VMEM((NYH * NYL, OUT_ROWS, WIDTH), jnp.float32),
        pltpu.VMEM((NYH * NYL, OUT_ROWS, WIDTH), jnp.bfloat16),
    ]
    for count in (NZ, NZ, slots, 2 * NX, slots, slots, NX, NYH * NYL):
        scratch += [dma((count,)), dma((count,))]
    return pl.pallas_call(
        head_kernel,
        out_shape=(
            jax.ShapeDtypeStruct((1, ROWS), jnp.float32),
            jax.ShapeDtypeStruct((OUT_ROWS, WIDTH), jnp.float32),
        ),
        in_specs=[vmem] * 5,
        out_specs=(vmem, vmem),
        scratch_shapes=scratch,
        compiler_params=pltpu.CompilerParams(
            collective_id=0, has_side_effects=True, vmem_limit_bytes=48 * 1024 * 1024
        ),
    )(unit_feats, labels, class_rows, unit_own, inverse_own)


def per_device(features, labels, weights, sampled):
    dp = lax.axis_index("dp")
    core, yl = dp % NCORE, dp // NCORE
    feat_wide = features.astype(jnp.float32)
    unit_feats = (feat_wide * normalize_rows(feat_wide)).astype(jnp.bfloat16)
    picked = lax.dynamic_index_in_dim(
        sampled.reshape(NYL, NCORE, OUT_ROWS), core, axis=1, keepdims=False
    ).reshape(ROWS)
    chosen = weights[picked]
    inverse_norm = normalize_rows(chosen)
    unit_f32 = chosen * inverse_norm
    unit_own = lax.dynamic_slice_in_dim(unit_f32, yl * OUT_ROWS, OUT_ROWS)
    inverse_own = lax.dynamic_slice_in_dim(inverse_norm, yl * OUT_ROWS, OUT_ROWS)
    loss, grad = head(
        unit_feats,
        labels.reshape(1, ROWS),
        unit_f32.astype(jnp.bfloat16),
        unit_own,
        inverse_own,
    )
    return (loss.reshape(ROWS), grad)


def solution(mesh):
    in_specs = (P(("cls", "dp"), None), P(("cls", "dp")), P("cls", None), P("cls"))
    out_specs = (P(("cls", "dp")), P(("cls", "dp"), None))
    return jax.shard_map(
        per_device, mesh=mesh, in_specs=in_specs, out_specs=out_specs, check_vma=False
    )
```

time: 777 us -> 74.6 us (0.10)
  blocking collectives: 374 us -> 0 us
  waiting for transfers between devices: 241 us -> 0 us
  Pallas kernels: 0 us -> 68.9 us
  matrix products: 57.7 us -> 0 us
  local copies, waits for them, and re-layouts: 49 us -> 3.65 us
  starting transfers between devices: 24.3 us -> 0 us
  between operations: 14.4 us -> 0.74 us
  other arithmetic: 9.74 us -> 0.35 us
    psum x1 -> x0, blocking collectives: 374 us -> none  [per_device(): totals = lax.psum(part_sum, 'cls')]
    all_gather x1 -> x0, waiting for transfers between devices: 158 us -> none  [per_device(): gathered = lax.all_gather(unit_feats, 'cls', axis=0, tiled=True)]
    pallas_call x0 -> x1, Pallas kernels: none -> 68.9 us  [head(): pl.pallas_call(head_kernel, out_shape=(jax.ShapeDtypeStruct((1, ROWS), jn...]
    reduce_scatter x1 -> x0, waiting for transfers between devices: 59.4 us -> none  [per_device(): lax.psum_scatter(inverse_norm * (unit_grad - unit_f32 * radial), 'dp', sc...]
    dot_general x32 -> x0, matrix products: 57.7 us -> none  [the longest x16 34.6 us: accumulate(): jnp.dot(grads_low.T, triple[0], preferred_element_type=jnp.float32)]
    all_to_all x2 -> x0, starting transfers between devices: 24.2 us -> none  [the longest x1 19.6 us: per_device(): lax.all_to_all(outgoing, 'cls', split_axis=0, concat_axis=0, tiled=True)]
    all_to_all x2 -> x0, waiting for transfers between devices: 23.6 us -> none  [the longest x1 13.1 us: per_device(): lax.all_to_all(values, 'cls', split_axis=0, concat_axis=0, tiled=True)]
    dynamic_update_slice x16 -> x0, local copies, waits for them, and re-layouts: 21.5 us -> none  [per_device(): part_sum, part_target = lax.map(first_pass, (feat_blocks, label_blocks))]
  transfers between devices with their start and end apart: 4 -> 0, of which waited for: 4 -> 0; matrix products, arithmetic and copies ran while one was open for 2% -> 0% of each run, Pallas kernels for 0% -> 0%
where the time goes in v1:
time: 74.6 us; the launch traced here: 73.6 us
  Pallas kernels  68.9 us (92%)
  local copies, waits for them, and re-layouts  3.65 us (5%)
    pallas_call x1, Pallas kernels, head(): pl.pallas_call(head_kernel, out_shape=(jax.ShapeDtypeStruct((1, ROWS), jn...  68.9 us
    unnamed x8, local copies, waits for them, and re-layouts  1.7 us

profile of v1, /device:TPU:1, one launch (start us, length us, event | category | flops | bytes accessed | tf_op | source)
XLA Modules:
  0.0 73.6 jit_solution(11556361080171348041)
XLA Ops:
  0.6 0.0 copy-start
  0.6 0.0 copy-start.2
  0.7 0.0 copy-start.1
  0.7 0.9 %reshape.68 = s32[4,2,32]{2,1,0:T(2,128)S(1)} reshape(s32[256]{0:T(256)} %param.7) | data formatting | bytes 2048 | tf_op jit(solution)/shard_map/reshape | solution.py:369
  1.6 0.1 reshape.69
  1.7 0.5 copy-done
  2.2 0.8 %gather_fusion = f32[128,512]{1,0:T(8,128)S(1)} fusion(f32[1024,512]{1,0:T(8,128)S(1)} %copy-done, s32[1024]{0:T(1024)S(1)} %pad_clamp_fusion), kind=kCustom, calls=%fused_computation | custom fusion | bytes 524800 | tf_op jit(solution)/shard_map/gather | solution.py:371
  3.0 0.1 multiply_reduce_fusion
  3.1 0.0 copy-done.2
  3.1 0.1 fusion
  3.3 0.1 fusion.3
  3.4 0.1 dynamic-slice_bitcast_fusion
  3.5 0.1 copy.7.inverse_ref
  3.6 0.0 copy-done.1
  3.6 68.9 %shard_map.59 = (f32[1,128]{1,0:T(1,128)S(1)}, f32[32,512]{1,0:T(8,128)S(1)}) custom-call(bf16[128,512]{1,0:T(8,128)(2,1)S(1)} %get-tuple-element.8.feat_ref, s32[1,128]{1,0:T(1,128)S(1)} %bitcast.6, bf16[128,512]{1,0:T(8,128)(2,1)S(1)} %get-tuple-element.6.class_ref, f32[32,512]{1,0:T(8,128)S(1)} %constant_dynamic-slice_fusion.unit_ref, ...), custom_call_target="tpu_custom_call" | custom-call | tf_op jit(solution)/shard_map/pallas_call | solution.py:348
  72.5 0.5 copy.10
  73.0 0.6 copy.11
  (6 shorter events, 0.1 us)
Async XLA Ops:
  0.6 1.6 %copy-start = (f32[1024,512]{1,0:T(8,128)S(1)}, f32[1024,512]{1,0:T(8,128)}, u32[]{:S(2)}) copy-start(f32[1024,512]{1,0:T(8,128)} %param.6) | copy-start | bytes 6291460
  0.6 2.5 %copy-start.2 = (bf16[128,512]{1,0:T(8,128)(2,1)S(1)}, bf16[128,512]{1,0:T(8,128)(2,1)}, u32[]{:S(2)}) copy-start(bf16[128,512]{1,0:T(8,128)(2,1)} %param.4) | copy-start | bytes 393220
  0.7 2.9 %copy-start.1 = (s32[128]{0:T(128)S(1)}, s32[128]{0:T(128)}, u32[]{:S(2)}) copy-start(s32[128]{0:T(128)} %param.5) | copy-start | bytes 1540

commit v2 on v1

v2 whole, which is shorter than its diff:
```python
import functools

import jax
import jax.numpy as jnp
from jax import lax
from jax.experimental import pallas as pl
from jax.experimental.pallas import tpu as pltpu
from jax.sharding import PartitionSpec as P

logit_scale = 64.0
margin = 0.35
epsilon = 1e-06

NX, NZ, NYH, NYL, NCORE = 4, 8, 2, 4, 2
ROWS = 128
OUT_ROWS = 32
WIDTH = 512
PAIR = 2 * ROWS
HALF = ROWS // 2
BANKS = NX * ROWS
EAST = 384
NORTH = WIDTH - EAST


def normalize_rows(matrix):
    squares = jnp.sum(matrix * matrix, axis=1, keepdims=True)
    return lax.rsqrt(squares + epsilon)


def head_kernel(
    feat_ref,
    label_ref,
    class_ref,
    unit_ref,
    inverse_ref,
    loss_ref,
    grad_ref,
    feats,
    classes,
    labels,
    ids,
    probs,
    grads,
    inverse_total,
    sums,
    sums_in,
    targets,
    targets_in,
    part_out,
    part_in,
    part_own,
    half_out,
    half_own,
    half_in,
    north_out,
    north_own,
    north_in,
    last_out,
    last_in,
    feat_send,
    feat_recv,
    core_send,
    core_recv,
    label_send,
    label_recv,
    class_send,
    class_recv,
    sum_send,
    sum_recv,
    target_send,
    target_recv,
    part_send,
    part_recv,
    half_send,
    half_recv,
    north_send,
    north_recv,
    last_send,
    last_recv,
):
    cls, dp = lax.axis_index("cls"), lax.axis_index("dp")
    x, z, yh = lax.div(cls, 16), lax.rem(lax.div(cls, 2), 8), lax.rem(cls, 2)
    yl, core = lax.div(dp, 2), lax.rem(dp, 2)

    def device(dx=0, dz=0, dyh=0, dyl=0, dcore=0):
        px = lax.rem(x + dx, NX)
        pz = lax.rem(z + dz, NZ)
        pyh = lax.rem(yh + dyh, NYH)
        pyl = lax.rem(yl + dyl, NYL)
        pcore = lax.rem(core + dcore, NCORE)
        return ((px * NZ + pz) * NYH + pyh, pyl * NCORE + pcore)

    mirror = ((x * NZ + z) * NYH + (1 - yh), (NYL - 1 - yl) * NCORE + core)

    def copy(src, dst, send, recv, target):
        return pltpu.make_async_remote_copy(
            src_ref=src,
            dst_ref=dst,
            send_sem=send,
            recv_sem=recv,
            device_id=target,
            device_id_type=pl.DeviceIdType.MESH,
        )

    plane = [(o, w) for o in range(NZ) for w in range(NCORE) if (o, w) != (0, 0)]
    column = [(u, v) for u in range(NYH) for v in range(NYL) if (u, v) != (0, 0)]

    barrier = pltpu.get_barrier_semaphore()
    peers = [device(dz=o, dcore=w) for o, w in plane]
    peers += [device(dx=i) for i in range(1, NX)]
    peers += [device(dyh=u, dyl=v) for u, v in column]
    for peer in peers:
        pl.semaphore_signal(barrier, inc=1, device_id=peer, device_id_type=pl.DeviceIdType.MESH)
    pl.semaphore_wait(barrier, len(peers))

    def feat_copy(slot, h):
        if slot <= NZ // 2:
            came, target = slot - 1, device(dz=1)
        else:
            came, target = (slot + 1) % NZ, device(dz=NZ - 1)
        rows = pl.ds(h * HALF, HALF)
        src = feat_ref.at[rows] if came == 0 else feats.at[came, rows]
        k = 2 * slot + h
        return copy(src, feats.at[slot, rows], feat_send.at[k], feat_recv.at[k], target)

    def core_copy(slot, h):
        rows = pl.ds(h * HALF, HALF)
        src = feat_ref.at[rows] if slot == 0 else feats.at[slot, rows]
        k = 2 * slot + h
        return copy(
            src,
            feats.at[slot, pl.ds(ROWS + h * HALF, HALF)],
            core_send.at[k],
            core_recv.at[k],
            device(dcore=1),
        )

    def class_copy(i, u, h):
        rows = pl.ds(i * ROWS + h * HALF, HALF)
        near = pl.ds(h * HALF, HALF)
        if i == 0:
            src, target = class_ref.at[near], mirror
        else:
            src = class_ref.at[near] if u == 0 else classes.at[1, near]
            target = device(dx=i)
        k = 4 * i + 2 * u + h
        return copy(src, classes.at[u, rows], class_send.at[k], class_recv.at[k], target)

    def label_copy(o, w):
        k = 2 * o + w
        return copy(
            label_ref, labels.at[k], label_send.at[k], label_recv.at[k], device(dz=o, dcore=w)
        )

    feat_copies = {(s, h): feat_copy(s, h) for s in range(1, NZ) for h in range(2)}
    core_copies = {(s, h): core_copy(s, h) for s in range(NZ) for h in range(2)}
    class_copies = {
        (i, u, h): class_copy(i, u, h)
        for i in range(NX)
        for u in range(2)
        for h in range(2)
        if i + u
    }
    label_copies = [label_copy(o, w) for o, w in plane]

    for h in range(2):
        class_copies[0, 1, h].start()
        feat_copies[1, h].start()
        feat_copies[NZ - 1, h].start()
    for i in (2, 1, 3):
        for h in range(2):
            class_copies[i, 0, h].start()
    for h in range(2):
        core_copies[0, h].start()
    for one in label_copies:
        one.start()

    feats[0, :ROWS] = feat_ref[...]
    classes[0, :ROWS] = class_ref[...]
    labels[0] = label_ref[...]
    sums[...] = jnp.zeros_like(sums)
    targets[...] = jnp.zeros_like(targets)
    row = lax.broadcasted_iota(jnp.int32, (ROWS, PAIR), 0)
    within = (
        lax.shift_right_logical(row, 5) * (2 * OUT_ROWS)
        + lax.bitwise_and(row, OUT_ROWS - 1)
        + (z * (2 * PAIR) + core * OUT_ROWS)
    )
    for i in range(NX):
        bank = lax.rem(x + (NX - i), NX) * (NZ * NYH * PAIR)
        ids[0, i * ROWS : (i + 1) * ROWS] = within + (bank + yh * PAIR)
        ids[1, i * ROWS : (i + 1) * ROWS] = within + (bank + (1 - yh) * PAIR)

    def names(s):
        return jnp.concatenate([labels[2 * s], labels[2 * s + 1]], axis=1)

    def first_pass(s, u):
        cosine = lax.dot_general(
            classes[u],
            feats[s],
            (((1,), (1,)), ((), ())),
            preferred_element_type=jnp.float32,
        )
        hit = ids[u] == names(s)
        logits = logit_scale * (cosine - jnp.where(hit, margin, 0.0))
        prob = jnp.exp(logits - logit_scale)
        probs[u, s] = prob
        total = jnp.sum(prob, axis=0, keepdims=True)
        target = jnp.sum(jnp.where(hit, logits, 0.0), axis=0, keepdims=True)
        sums[0, pl.ds(s, 1)] += total[:, :ROWS]
        sums[1, pl.ds(s, 1)] += total[:, ROWS:]
        targets[2 * s] += target[:, :ROWS]
        targets[2 * s + 1] += target[:, ROWS:]

    def receive_features(step):
        for h in range(2):
            feat_copies[step, h].wait_recv()
            if step < NZ // 2:
                feat_copies[step + 1, h].start()
            core_copies[step, h].start()
            if step < NZ // 2:
                back = NZ - step
                feat_copies[back, h].wait_recv()
                if step < NZ // 2 - 1:
                    feat_copies[back - 1, h].start()
                core_copies[back, h].start()
            if step == 2:
                class_copies[0, 1, h].wait_recv()
                for i in (2, 1, 3):
                    class_copies[i, 1, h].start()

    def receive_cores(*slots):
        for slot in slots:
            for h in range(2):
                core_copies[slot, h].wait_recv()

    def receive_classes(u):
        for i in range(1, NX):
            for h in range(2):
                class_copies[i, u, h].wait_recv()

    receive_features(1)
    receive_features(2)
    receive_classes(0)
    for one in label_copies:
        one.wait_recv()
    receive_cores(0, 1, 7)

    @pl.loop(0, 3)
    def _(k):
        first_pass(lax.rem(k + (NZ - 1), NZ), 0)

    receive_features(3)
    receive_cores(2, 6, 3, 5)

    @pl.loop(0, 4)
    def _(k):
        first_pass(2 + lax.div(k, 2) + lax.rem(k, 2) * (NZ - 4 - 2 * lax.div(k, 2)), 0)

    receive_features(4)
    receive_classes(1)
    receive_cores(4)

    @pl.loop(0, NZ + 1)
    def _(k):
        near = lax.div(NZ - k, NZ)
        first_pass(near * (NZ // 2) + (1 - near) * (k - 1), 1 - near)

    sum_copies, target_copies = {}, {}
    for o, w in plane:
        k = 2 * o + w
        sum_copies[o, w] = copy(
            sums, sums_in.at[k], sum_send.at[k], sum_recv.at[k], device(dz=o, dcore=w)
        )
        target_copies[o, w] = copy(
            targets.at[k],
            targets_in.at[k],
            target_send.at[k],
            target_recv.at[k],
            device(dz=NZ - o, dcore=w),
        )
    for one in sum_copies.values():
        one.start()
    for one in target_copies.values():
        one.start()
    whole = [sums[0], sums[1]]
    for (o, w), one in sum_copies.items():
        one.wait_recv()
        for q in range(2):
            other = sums_in[2 * o + w, (q + w) % 2]
            whole[q] += other if o == 0 else pltpu.roll(other, o, 0)
    for q in range(2):
        inverse_total[q] = 1.0 / whole[q]

    part_copies, north_copies = {}, {}
    for i in (2, 1, 3, 0):

        def weigh(s, carry):
            inverse = jnp.concatenate(
                [inverse_total[0, pl.ds(s, 1)], inverse_total[1, pl.ds(s, 1)]], axis=1
            )
            name = names(s)
            for u in range(2):
                rows = pl.ds(i * ROWS, ROWS)
                hit = jnp.where(ids[u, rows] == name, 1.0, 0.0)
                slope = probs[u, s, rows] * inverse - hit
                grads[s, u * ROWS : (u + 1) * ROWS] = slope.astype(jnp.bfloat16)
            return carry

        lax.fori_loop(0, NZ, weigh, 0)
        part = jnp.zeros((PAIR, WIDTH), jnp.float32)
        for s in range(NZ):
            part += jnp.dot(grads[s], feats[s], preferred_element_type=jnp.float32)
        north = part[:, EAST:].reshape(NYH * NYL, OUT_ROWS, NORTH)
        north_own[i] = north
        north_out[i] = north.astype(jnp.bfloat16)
        if i == 0:
            part_own[...] = part[:, :EAST]
        else:
            part_out[i] = part[:, :EAST].astype(jnp.bfloat16)
            part_copies[i] = copy(
                part_out.at[i],
                part_in.at[i],
                part_send.at[i],
                part_recv.at[i],
                device(dx=NX - i),
            )
            part_copies[i].start()
        for u, v in column:
            k = NYL * u + v
            north_copies[i, k] = copy(
                north_out.at[i, NYL * u + lax.rem(yl + v, NYL)],
                north_in.at[i, k],
                north_send.at[NX * k + i],
                north_recv.at[NX * k + i],
                device(dyh=u, dyl=v),
            )
            north_copies[i, k].start()

    own_target = targets[0]
    for (o, w), one in target_copies.items():
        one.wait_recv()
        own_target += targets_in[2 * o + w]
    loss_ref[...] = logit_scale + jnp.log(whole[0][0:1]) - own_target

    last_copies = {}
    for i in (2, 1, 3, 0):
        north = north_own[i, yl]
        for k in range(1, NYH * NYL):
            north_copies[i, k].wait_recv()
            north += north_in[i, k].astype(jnp.float32)
        if i > 0:
            last_out[i] = north.astype(jnp.bfloat16)
            last_copies[i] = copy(
                last_out.at[i],
                last_in.at[i],
                last_send.at[i],
                last_recv.at[i],
                device(dx=NX - i),
            )
            last_copies[i].start()

    half = part_own[...]
    for i in (1, 3, 2):
        part_copies[i].wait_recv()
        half += part_in[i].astype(jnp.float32)
    half = half.reshape(NYH * NYL, OUT_ROWS, EAST)
    half_own[...] = half
    half_out[...] = half.astype(jnp.bfloat16)
    half_copies = {}
    for u, v in column:
        k = NYL * u + v
        half_copies[u, v] = copy(
            half_out.at[NYL * u + lax.rem(yl + v, NYL)],
            half_in.at[k],
            half_send.at[k],
            half_recv.at[k],
            device(dyh=u, dyl=v),
        )
        half_copies[u, v].start()
    for i, one in last_copies.items():
        one.wait_recv()
        north += last_in[i].astype(jnp.float32)
    east = half_own[yl]
    for (u, v), one in half_copies.items():
        one.wait_recv()
        east += half_in[NYL * u + v].astype(jnp.float32)
    total = (logit_scale / 8.0) * jnp.concatenate([east, north], axis=1)
    unit = unit_ref[...]
    radial = jnp.sum(unit * total, axis=1, keepdims=True)
    grad_ref[...] = inverse_ref[...] * (total - unit * radial)

    for group in (
        feat_copies,
        core_copies,
        class_copies,
        sum_copies,
        target_copies,
        part_copies,
        half_copies,
        north_copies,
        last_copies,
    ):
        for one in group.values():
            one.wait_send()
    for one in label_copies:
        one.wait_send()


def head(unit_feats, labels, class_rows, unit_own, inverse_own):
    vmem = pl.BlockSpec(memory_space=pltpu.VMEM)
    dma = pltpu.SemaphoreType.DMA
    slots, column = NZ * NCORE, NYH * NYL
    scratch = [
        pltpu.VMEM((NZ, PAIR, WIDTH), jnp.bfloat16),
        pltpu.VMEM((2, BANKS, WIDTH), jnp.bfloat16),
        pltpu.VMEM((slots, 1, ROWS), jnp.int32),
        pltpu.VMEM((2, BANKS, PAIR), jnp.int32),
        pltpu.VMEM((2, NZ, BANKS, PAIR), jnp.float32),
        pltpu.VMEM((NZ, PAIR, PAIR), jnp.bfloat16),
        pltpu.VMEM((2, NZ, ROWS), jnp.float32),
        pltpu.VMEM((2, NZ, ROWS), jnp.float32),
        pltpu.VMEM((slots, 2, NZ, ROWS), jnp.float32),
        pltpu.VMEM((slots, 1, ROWS), jnp.float32),
        pltpu.VMEM((slots, 1, ROWS), jnp.float32),
        pltpu.VMEM((NX, PAIR, EAST), jnp.bfloat16),
        pltpu.VMEM((NX, PAIR, EAST), jnp.bfloat16),
        pltpu.VMEM((PAIR, EAST), jnp.float32),
        pltpu.VMEM((column, OUT_ROWS, EAST), jnp.bfloat16),
        pltpu.VMEM((column, OUT_ROWS, EAST), jnp.float32),
        pltpu.VMEM((column, OUT_ROWS, EAST), jnp.bfloat16),
        pltpu.VMEM((NX, column, OUT_ROWS, NORTH), jnp.bfloat16),
        pltpu.VMEM((NX, column, OUT_ROWS, NORTH), jnp.float32),
        pltpu.VMEM((NX, column, OUT_ROWS, NORTH), jnp.bfloat16),
        pltpu.VMEM((NX, OUT_ROWS, NORTH), jnp.bfloat16),
        pltpu.VMEM((NX, OUT_ROWS, NORTH), jnp.bfloat16),
    ]
    counts = (2 * NZ, 2 * NZ, slots, 4 * NX, slots, slots, NX, column, NX * column, NX)
    for count in counts:
        scratch += [dma((count,)), dma((count,))]
    return pl.pallas_call(
        head_kernel,
        out_shape=(
            jax.ShapeDtypeStruct((1, ROWS), jnp.float32),
            jax.ShapeDtypeStruct((OUT_ROWS, WIDTH), jnp.float32),
        ),
        in_specs=[vmem] * 5,
        out_specs=(vmem, vmem),
        scratch_shapes=scratch,
        compiler_params=pltpu.CompilerParams(
            collective_id=0, has_side_effects=True, vmem_limit_bytes=48 * 1024 * 1024
        ),
    )(unit_feats, labels, class_rows, unit_own, inverse_own)


def per_device(features, labels, weights, sampled):
    dp = lax.axis_index("dp")
    core, yl = dp % NCORE, dp // NCORE
    feat_wide = features.astype(jnp.float32)
    unit_feats = (feat_wide * normalize_rows(feat_wide)).astype(jnp.bfloat16)
    picked = lax.dynamic_index_in_dim(
        sampled.reshape(NYL, NCORE, OUT_ROWS), core, axis=1, keepdims=False
    ).reshape(ROWS)
    chosen = weights[picked]
    inverse_norm = normalize_rows(chosen)
    unit_f32 = chosen * inverse_norm
    unit_own = lax.dynamic_slice_in_dim(unit_f32, yl * OUT_ROWS, OUT_ROWS)
    inverse_own = lax.dynamic_slice_in_dim(inverse_norm, yl * OUT_ROWS, OUT_ROWS)
    loss, grad = head(
        unit_feats,
        labels.reshape(1, ROWS),
        unit_f32.astype(jnp.bfloat16),
        unit_own,
        inverse_own,
    )
    return (loss.reshape(ROWS), grad)


def solution(mesh):
    in_specs = (P(("cls", "dp"), None), P(("cls", "dp")), P("cls", None), P("cls"))
    out_specs = (P(("cls", "dp")), P(("cls", "dp"), None))
    return jax.shard_map(
        per_device, mesh=mesh, in_specs=in_specs, out_specs=out_specs, check_vma=False
    )
```

time: 74.6 us -> 71.3 us (0.956); the launches traced: 73.6 us -> 71.1 us
  Pallas kernels: 68.9 us -> 66.4 us
    pallas_call x1, Pallas kernels: 68.9 us -> 66.4 us  [head(): pl.pallas_call(head_kernel, out_shape=(jax.ShapeDtypeStruct((1, ROWS), jn...]
where the time goes in v2:
time: 71.3 us; the launch traced here: 71.1 us
  Pallas kernels  66.4 us (93%)
  local copies, waits for them, and re-layouts  3.65 us (5%)
  between operations  0.74 us (1%)
    pallas_call x1, Pallas kernels, head(): pl.pallas_call(head_kernel, out_shape=(jax.ShapeDtypeStruct((1, ROWS), jn...  66.4 us
    unnamed x8, local copies, waits for them, and re-layouts  1.7 us

profile of v2, /device:TPU:1, one launch (start us, length us, event | category | flops | bytes accessed | tf_op | source)
XLA Modules:
  0.0 71.1 jit_solution(540709051169306559)
XLA Ops:
  0.6 0.0 copy-start
  0.6 0.0 copy-start.2
  0.7 0.0 copy-start.1
  0.7 0.9 %reshape.68 = s32[4,2,32]{2,1,0:T(2,128)S(1)} reshape(s32[256]{0:T(256)} %param.7) | data formatting | bytes 2048 | tf_op jit(solution)/shard_map/reshape | solution.py:462
  1.6 0.1 reshape.69
  1.7 0.5 copy-done
  2.2 0.8 %gather_fusion = f32[128,512]{1,0:T(8,128)S(1)} fusion(f32[1024,512]{1,0:T(8,128)S(1)} %copy-done, s32[1024]{0:T(1024)S(1)} %pad_clamp_fusion), kind=kCustom, calls=%fused_computation | custom fusion | bytes 524800 | tf_op jit(solution)/shard_map/gather | solution.py:464
  3.0 0.1 multiply_reduce_fusion
  3.1 0.0 copy-done.2
  3.1 0.1 fusion
  3.3 0.1 fusion.3
  3.4 0.1 dynamic-slice_bitcast_fusion
  3.5 0.1 copy.7.inverse_ref
  3.6 0.0 copy-done.1
  3.6 66.4 %shard_map.59 = (f32[1,128]{1,0:T(1,128)S(1)}, f32[32,512]{1,0:T(8,128)S(1)}) custom-call(bf16[128,512]{1,0:T(8,128)(2,1)S(1)} %get-tuple-element.8.feat_ref, s32[1,128]{1,0:T(1,128)S(1)} %bitcast.6, bf16[128,512]{1,0:T(8,128)(2,1)S(1)} %get-tuple-element.6.class_ref, f32[32,512]{1,0:T(8,128)S(1)} %constant_dynamic-slice_fusion.unit_ref, ...), custom_call_target="tpu_custom_call" | custom-call | tf_op jit(solution)/shard_map/pallas_call | solution.py:441
  70.0 0.5 copy.10
  70.5 0.6 copy.11
  (6 shorter events, 0.1 us)
Async XLA Ops:
  0.6 1.6 %copy-start = (f32[1024,512]{1,0:T(8,128)S(1)}, f32[1024,512]{1,0:T(8,128)}, u32[]{:S(2)}) copy-start(f32[1024,512]{1,0:T(8,128)} %param.6) | copy-start | bytes 6291460
  0.6 2.5 %copy-start.2 = (bf16[128,512]{1,0:T(8,128)(2,1)S(1)}, bf16[128,512]{1,0:T(8,128)(2,1)}, u32[]{:S(2)}) copy-start(bf16[128,512]{1,0:T(8,128)(2,1)} %param.4) | copy-start | bytes 393220
  0.7 2.9 %copy-start.1 = (s32[128]{0:T(128)S(1)}, s32[128]{0:T(128)}, u32[]{:S(2)}) copy-start(s32[128]{0:T(128)} %param.5) | copy-start | bytes 1540

commit v3 on v2

--- a/solution.py
+++ b/solution.py
@@ -14,9 +14,11 @@
 NX, NZ, NYH, NYL, NCORE = 4, 8, 2, 4, 2
 ROWS = 128
 OUT_ROWS = 32
+BANK = 1024
 WIDTH = 512
 PAIR = 2 * ROWS
 HALF = ROWS // 2
+QUARTER = ROWS // 4
 BANKS = NX * ROWS
 EAST = 384
 NORTH = WIDTH - EAST
@@ -30,9 +32,8 @@
 def head_kernel(
     feat_ref,
     label_ref,
-    class_ref,
-    unit_ref,
-    inverse_ref,
+    bank_ref,
+    sampled_ref,
     loss_ref,
     grad_ref,
     feats,
@@ -57,6 +58,11 @@
     north_in,
     last_out,
     last_in,
+    feat_in,
+    places,
+    bank,
+    chosen,
+    load_sem,
     feat_send,
     feat_recv,
     core_send,
@@ -105,30 +111,42 @@
     plane = [(o, w) for o in range(NZ) for w in range(NCORE) if (o, w) != (0, 0)]
     column = [(u, v) for u in range(NYH) for v in range(NYL) if (u, v) != (0, 0)]
 
+    feat_load = pltpu.make_async_copy(feat_ref, feat_in, load_sem.at[0])
+    label_load = pltpu.make_async_copy(label_ref, labels.at[0], load_sem.at[1])
+    sampled_load = pltpu.make_async_copy(sampled_ref, places, load_sem.at[2])
+    bank_load = pltpu.make_async_copy(bank_ref, bank, load_sem.at[3])
+    for one in (feat_load, label_load, sampled_load, bank_load):
+        one.start()
     barrier = pltpu.get_barrier_semaphore()
     peers = [device(dz=o, dcore=w) for o, w in plane]
     peers += [device(dx=i) for i in range(1, NX)]
     peers += [device(dyh=u, dyl=v) for u, v in column]
     for peer in peers:
         pl.semaphore_signal(barrier, inc=1, device_id=peer, device_id_type=pl.DeviceIdType.MESH)
+    feat_load.wait()
+    feat_wide = feat_in[...].astype(jnp.float32)
+    feats[0, :ROWS] = (feat_wide * normalize_rows(feat_wide)).astype(jnp.bfloat16)
+    label_load.wait()
+    sums[...] = jnp.zeros_like(sums)
+    targets[...] = jnp.zeros_like(targets)
     pl.semaphore_wait(barrier, len(peers))
 
     def feat_copy(slot, h):
-        if slot <= NZ // 2:
+        if slot < NZ // 2 or (slot == NZ // 2 and h < 2):
             came, target = slot - 1, device(dz=1)
         else:
             came, target = (slot + 1) % NZ, device(dz=NZ - 1)
-        rows = pl.ds(h * HALF, HALF)
-        src = feat_ref.at[rows] if came == 0 else feats.at[came, rows]
-        k = 2 * slot + h
-        return copy(src, feats.at[slot, rows], feat_send.at[k], feat_recv.at[k], target)
+        rows = pl.ds(h * QUARTER, QUARTER)
+        k = 4 * slot + h
+        return copy(
+            feats.at[came, rows], feats.at[slot, rows], feat_send.at[k], feat_recv.at[k], target
+        )
 
     def core_copy(slot, h):
         rows = pl.ds(h * HALF, HALF)
-        src = feat_ref.at[rows] if slot == 0 else feats.at[slot, rows]
         k = 2 * slot + h
         return copy(
-            src,
+            feats.at[slot, rows],
             feats.at[slot, pl.ds(ROWS + h * HALF, HALF)],
             core_send.at[k],
             core_recv.at[k],
@@ -139,20 +157,20 @@
         rows = pl.ds(i * ROWS + h * HALF, HALF)
         near = pl.ds(h * HALF, HALF)
         if i == 0:
-            src, target = class_ref.at[near], mirror
+            target = mirror
         else:
-            src = class_ref.at[near] if u == 0 else classes.at[1, near]
             target = device(dx=i)
         k = 4 * i + 2 * u + h
+        src = classes.at[1 if i and u else 0, near]
         return copy(src, classes.at[u, rows], class_send.at[k], class_recv.at[k], target)
 
     def label_copy(o, w):
         k = 2 * o + w
         return copy(
-            label_ref, labels.at[k], label_send.at[k], label_recv.at[k], device(dz=o, dcore=w)
-        )
-
-    feat_copies = {(s, h): feat_copy(s, h) for s in range(1, NZ) for h in range(2)}
+            labels.at[0], labels.at[k], label_send.at[k], label_recv.at[k], device(dz=o, dcore=w)
+        )
+
+    feat_copies = {(s, h): feat_copy(s, h) for s in range(1, NZ) for h in range(4)}
     core_copies = {(s, h): core_copy(s, h) for s in range(NZ) for h in range(2)}
     class_copies = {
         (i, u, h): class_copy(i, u, h)
@@ -163,23 +181,26 @@
     }
     label_copies = [label_copy(o, w) for o, w in plane]
 
-    for h in range(2):
-        class_copies[0, 1, h].start()
+    for h in range(4):
         feat_copies[1, h].start()
         feat_copies[NZ - 1, h].start()
-    for i in (2, 1, 3):
-        for h in range(2):
-            class_copies[i, 0, h].start()
     for h in range(2):
         core_copies[0, h].start()
     for one in label_copies:
         one.start()
 
-    feats[0, :ROWS] = feat_ref[...]
-    classes[0, :ROWS] = class_ref[...]
-    labels[0] = label_ref[...]
-    sums[...] = jnp.zeros_like(sums)
-    targets[...] = jnp.zeros_like(targets)
+    sampled_load.wait()
+    bank_load.wait()
+
+    @pl.loop(0, ROWS // 8)
+    def _(block):
+        for r in range(8):
+            k = block * 8 + r
+            place = lax.div(k, OUT_ROWS) * (2 * OUT_ROWS) + core * OUT_ROWS + lax.rem(k, OUT_ROWS)
+            chosen[pl.ds(k, 1)] = bank[pl.ds(places[place], 1)]
+
+    picked = chosen[...]
+    classes[0, :ROWS] = (picked * normalize_rows(picked)).astype(jnp.bfloat16)
     row = lax.broadcasted_iota(jnp.int32, (ROWS, PAIR), 0)
     within = (
         lax.shift_right_logical(row, 5) * (2 * OUT_ROWS)
@@ -187,9 +208,14 @@
         + (z * (2 * PAIR) + core * OUT_ROWS)
     )
     for i in range(NX):
-        bank = lax.rem(x + (NX - i), NX) * (NZ * NYH * PAIR)
-        ids[0, i * ROWS : (i + 1) * ROWS] = within + (bank + yh * PAIR)
-        ids[1, i * ROWS : (i + 1) * ROWS] = within + (bank + (1 - yh) * PAIR)
+        base = lax.rem(x + (NX - i), NX) * (NZ * NYH * PAIR)
+        ids[0, i * ROWS : (i + 1) * ROWS] = within + (base + yh * PAIR)
+        ids[1, i * ROWS : (i + 1) * ROWS] = within + (base + (1 - yh) * PAIR)
+    for h in range(2):
+        class_copies[0, 1, h].start()
+    for i in (2, 1, 3):
+        for h in range(2):
+            class_copies[i, 0, h].start()
 
     def names(s):
         return jnp.concatenate([labels[2 * s], labels[2 * s + 1]], axis=1)
@@ -213,21 +239,27 @@
         targets[2 * s + 1] += target[:, ROWS:]
 
     def receive_features(step):
-        for h in range(2):
-            feat_copies[step, h].wait_recv()
+        back = NZ - step
+        for h in range(4):
             if step < NZ // 2:
-                feat_copies[step + 1, h].start()
-            core_copies[step, h].start()
-            if step < NZ // 2:
-                back = NZ - step
+                feat_copies[step, h].wait_recv()
+                if step + 1 < NZ // 2 or h < 2:
+                    feat_copies[step + 1, h].start()
                 feat_copies[back, h].wait_recv()
-                if step < NZ // 2 - 1:
+                if step + 1 < NZ // 2 or h >= 2:
                     feat_copies[back - 1, h].start()
-                core_copies[back, h].start()
-            if step == 2:
-                class_copies[0, 1, h].wait_recv()
+                if h % 2:
+                    core_copies[step, h // 2].start()
+                    core_copies[back, h // 2].start()
+            if step == 2 and h % 2:
+                class_copies[0, 1, h // 2].wait_recv()
                 for i in (2, 1, 3):
-                    class_copies[i, 1, h].start()
+                    class_copies[i, 1, h // 2].start()
+        if step == NZ // 2:
+            for h in (0, 2, 1, 3):
+                feat_copies[step, h].wait_recv()
+                if h in (1, 3):
+                    core_copies[step, h // 2].start()
 
     def receive_cores(*slots):
         for slot in slots:
@@ -257,14 +289,23 @@
     def _(k):
         first_pass(2 + lax.div(k, 2) + lax.rem(k, 2) * (NZ - 4 - 2 * lax.div(k, 2)), 0)
 
+    receive_classes(1)
+
+    @pl.loop(0, 3)
+    def _(k):
+        first_pass(lax.rem(k + (NZ - 1), NZ), 1)
+
     receive_features(4)
-    receive_classes(1)
+
+    @pl.loop(0, 4)
+    def _(k):
+        first_pass(2 + lax.div(k, 2) + lax.rem(k, 2) * (NZ - 4 - 2 * lax.div(k, 2)), 1)
+
     receive_cores(4)
 
-    @pl.loop(0, NZ + 1)
+    @pl.loop(0, 2)
     def _(k):
-        near = lax.div(NZ - k, NZ)
-        first_pass(near * (NZ // 2) + (1 - near) * (k - 1), 1 - near)
+        first_pass(NZ // 2, k)
 
     sum_copies, target_copies = {}, {}
     for o, w in plane:
@@ -386,9 +427,11 @@
         one.wait_recv()
         east += half_in[NYL * u + v].astype(jnp.float32)
     total = (logit_scale / 8.0) * jnp.concatenate([east, north], axis=1)
-    unit = unit_ref[...]
+    own = chosen[pl.ds(pl.multiple_of(yl * OUT_ROWS, OUT_ROWS), OUT_ROWS)]
+    inverse = normalize_rows(own)
+    unit = own * inverse
     radial = jnp.sum(unit * total, axis=1, keepdims=True)
-    grad_ref[...] = inverse_ref[...] * (total - unit * radial)
+    grad_ref[...] = inverse * (total - unit * radial)
 
     for group in (
         feat_copies,
@@ -407,7 +450,7 @@
         one.wait_send()
 
 
-def head(unit_feats, labels, class_rows, unit_own, inverse_own):
+def head(features, labels, weights, sampled):
     vmem = pl.BlockSpec(memory_space=pltpu.VMEM)
     dma = pltpu.SemaphoreType.DMA
     slots, column = NZ * NCORE, NYH * NYL
@@ -434,8 +477,13 @@
         pltpu.VMEM((NX, column, OUT_ROWS, NORTH), jnp.bfloat16),
         pltpu.VMEM((NX, OUT_ROWS, NORTH), jnp.bfloat16),
         pltpu.VMEM((NX, OUT_ROWS, NORTH), jnp.bfloat16),
+        pltpu.VMEM((ROWS, WIDTH), jnp.bfloat16),
+        pltpu.SMEM((PAIR,), jnp.int32),
+        pltpu.VMEM((BANK, WIDTH), jnp.float32),
+        pltpu.VMEM((ROWS, WIDTH), jnp.float32),
+        dma((4,)),
     ]
-    counts = (2 * NZ, 2 * NZ, slots, 4 * NX, slots, slots, NX, column, NX * column, NX)
+    counts = (4 * NZ, 2 * NZ, slots, 4 * NX, slots, slots, NX, column, NX * column, NX)
     for count in counts:
         scratch += [dma((count,)), dma((count,))]
     return pl.pallas_call(
@@ -444,35 +492,15 @@
             jax.ShapeDtypeStruct((1, ROWS), jnp.float32),
             jax.ShapeDtypeStruct((OUT_ROWS, WIDTH), jnp.float32),
         ),
-        in_specs=[vmem] * 5,
+        in_specs=[pl.BlockSpec(memory_space=pl.ANY)] * 4,
         out_specs=(vmem, vmem),
         scratch_shapes=scratch,
-        compiler_params=pltpu.CompilerParams(
-            collective_id=0, has_side_effects=True, vmem_limit_bytes=48 * 1024 * 1024
-        ),
-    )(unit_feats, labels, class_rows, unit_own, inverse_own)
+        compiler_params=pltpu.CompilerParams(collective_id=0, has_side_effects=True),
+    )(features, labels, weights, sampled)
 
 
 def per_device(features, labels, weights, sampled):
-    dp = lax.axis_index("dp")
-    core, yl = dp % NCORE, dp // NCORE
-    feat_wide = features.astype(jnp.float32)
-    unit_feats = (feat_wide * normalize_rows(feat_wide)).astype(jnp.bfloat16)
-    picked = lax.dynamic_index_in_dim(
-        sampled.reshape(NYL, NCORE, OUT_ROWS), core, axis=1, keepdims=False
-    ).reshape(ROWS)
-    chosen = weights[picked]
-    inverse_norm = normalize_rows(chosen)
-    unit_f32 = chosen * inverse_norm
-    unit_own = lax.dynamic_slice_in_dim(unit_f32, yl * OUT_ROWS, OUT_ROWS)
-    inverse_own = lax.dynamic_slice_in_dim(inverse_norm, yl * OUT_ROWS, OUT_ROWS)
-    loss, grad = head(
-        unit_feats,
-        labels.reshape(1, ROWS),
-        unit_f32.astype(jnp.bfloat16),
-        unit_own,
-        inverse_own,
-    )
+    loss, grad = head(features, labels.reshape(1, ROWS), weights, sampled)
     return (loss.reshape(ROWS), grad)
 
 

time: 71.3 us -> 68 us (0.954)
  Pallas kernels: 66.4 us -> 64.6 us
  local copies, waits for them, and re-layouts: 3.65 us -> 2.59 us
    pallas_call x1, Pallas kernels: 66.4 us -> 64.6 us  [head(): pl.pallas_call(head_kernel, out_shape=(jax.ShapeDtypeStruct((1, ROWS), jn...]
    reshape x2 -> x0, local copies, waits for them, and re-layouts: 1 us -> none  [the longest x1 0.91 us: per_device(): sampled.reshape(NYL, NCORE, OUT_ROWS)]
    unnamed x8 -> x2, local copies, waits for them, and re-layouts: 1.7 us -> 2.59 us
    gather x1 -> x0, local copies, waits for them, and re-layouts: 0.75 us -> none  [per_device(): chosen = weights[picked]]
where the time goes in v3:
time: 68 us; the launch traced here: 67.8 us
  Pallas kernels  64.6 us (95%)
  local copies, waits for them, and re-layouts  2.59 us (4%)
    pallas_call x1, Pallas kernels, head(): pl.pallas_call(head_kernel, out_shape=(jax.ShapeDtypeStruct((1, ROWS), jn...  64.6 us
    unnamed x2, local copies, waits for them, and re-layouts  2.59 us

profile of v3, /device:TPU:1, one launch (start us, length us, event | category | flops | bytes accessed | tf_op | source)
XLA Modules:
  0.0 67.8 jit_solution(18079882186597123788)
XLA Ops:
  0.6 64.6 %shard_map.59 = (f32[1,128]{1,0:T(1,128)}, f32[32,512]{1,0:T(8,128)}) custom-call(bf16[128,512]{1,0:T(8,128)(2,1)} %feat_ref.1, s32[1,128]{1,0:T(1,128)} %bitcast.2, f32[1024,512]{1,0:T(8,128)} %bank_ref.1, s32[256]{0:T(256)} %sampled_ref.1), custom_call_target="tpu_custom_call" | custom-call | tf_op jit(solution)/shard_map/pallas_call | solution.py:489
  65.2 1.1 %copy.8 = f32[128]{0:T(128)} copy(f32[128]{0:T(128)} %bitcast.3) | data formatting | bytes 1024
  66.4 1.5 %copy.9 = f32[32,512]{1,0:T(8,128)} copy(f32[32,512]{1,0:T(8,128)} %get-tuple-element.9) | data formatting | bytes 131072

commit v4 on v3

--- a/solution.py
+++ b/solution.py
@@ -22,6 +22,7 @@
 BANKS = NX * ROWS
 EAST = 384
 NORTH = WIDTH - EAST
+EAST_CUTS = ((0, 256), (256, 128))
 
 
 def normalize_rows(matrix):
@@ -334,6 +335,18 @@
         inverse_total[q] = 1.0 / whole[q]
 
     part_copies, north_copies = {}, {}
+
+    def send_part(turn, i):
+        columns = pl.ds(*EAST_CUTS[turn])
+        part_copies[turn, i] = copy(
+            part_out.at[i, :, columns],
+            part_in.at[i, :, columns],
+            part_send.at[NX * turn + i],
+            part_recv.at[NX * turn + i],
+            device(dx=NX - i),
+        )
+        part_copies[turn, i].start()
+
     for i in (2, 1, 3, 0):
 
         def weigh(s, carry):
@@ -359,14 +372,7 @@
             part_own[...] = part[:, :EAST]
         else:
             part_out[i] = part[:, :EAST].astype(jnp.bfloat16)
-            part_copies[i] = copy(
-                part_out.at[i],
-                part_in.at[i],
-                part_send.at[i],
-                part_recv.at[i],
-                device(dx=NX - i),
-            )
-            part_copies[i].start()
+            send_part(0, i)
         for u, v in column:
             k = NYL * u + v
             north_copies[i, k] = copy(
@@ -377,6 +383,9 @@
                 device(dyh=u, dyl=v),
             )
             north_copies[i, k].start()
+
+    for i in (2, 1, 3):
+        send_part(1, i)
 
     own_target = targets[0]
     for (o, w), one in target_copies.items():
@@ -401,32 +410,39 @@
             )
             last_copies[i].start()
 
-    half = part_own[...]
-    for i in (1, 3, 2):
-        part_copies[i].wait_recv()
-        half += part_in[i].astype(jnp.float32)
-    half = half.reshape(NYH * NYL, OUT_ROWS, EAST)
-    half_own[...] = half
-    half_out[...] = half.astype(jnp.bfloat16)
     half_copies = {}
-    for u, v in column:
-        k = NYL * u + v
-        half_copies[u, v] = copy(
-            half_out.at[NYL * u + lax.rem(yl + v, NYL)],
-            half_in.at[k],
-            half_send.at[k],
-            half_recv.at[k],
-            device(dyh=u, dyl=v),
-        )
-        half_copies[u, v].start()
+    for turn, (start, width) in enumerate(EAST_CUTS):
+        columns = slice(start, start + width)
+        half = part_own[:, columns]
+        for i in (1, 3, 2):
+            part_copies[turn, i].wait_recv()
+            half += part_in[i, :, columns].astype(jnp.float32)
+        half = half.reshape(NYH * NYL, OUT_ROWS, width)
+        half_own[:, :, columns] = half
+        half_out[:, :, columns] = half.astype(jnp.bfloat16)
+        for u, v in column:
+            k = NYL * u + v
+            half_copies[turn, k] = copy(
+                half_out.at[NYL * u + lax.rem(yl + v, NYL), :, pl.ds(start, width)],
+                half_in.at[k, :, pl.ds(start, width)],
+                half_send.at[NYH * NYL * turn + k],
+                half_recv.at[NYH * NYL * turn + k],
+                device(dyh=u, dyl=v),
+            )
+            half_copies[turn, k].start()
     for i, one in last_copies.items():
         one.wait_recv()
         north += last_in[i].astype(jnp.float32)
-    east = half_own[yl]
-    for (u, v), one in half_copies.items():
-        one.wait_recv()
-        east += half_in[NYL * u + v].astype(jnp.float32)
-    total = (logit_scale / 8.0) * jnp.concatenate([east, north], axis=1)
+    pieces = []
+    for turn, (start, width) in enumerate(EAST_CUTS):
+        columns = slice(start, start + width)
+        piece = half_own[yl, :, columns]
+        for k in range(1, NYH * NYL):
+            half_copies[turn, k].wait_recv()
+            piece += half_in[k, :, columns].astype(jnp.float32)
+        pieces.append(piece)
+    pieces.append(north)
+    total = (logit_scale / 8.0) * jnp.concatenate(pieces, axis=1)
     own = chosen[pl.ds(pl.multiple_of(yl * OUT_ROWS, OUT_ROWS), OUT_ROWS)]
     inverse = normalize_rows(own)
     unit = own * inverse
@@ -483,7 +499,7 @@
         pltpu.VMEM((ROWS, WIDTH), jnp.float32),
         dma((4,)),
     ]
-    counts = (4 * NZ, 2 * NZ, slots, 4 * NX, slots, slots, NX, column, NX * column, NX)
+    counts = (4 * NZ, 2 * NZ, slots, 4 * NX, slots, slots, 2 * NX, 2 * column, NX * column, NX)
     for count in counts:
         scratch += [dma((count,)), dma((count,))]
     return pl.pallas_call(
@@ -492,10 +508,12 @@
             jax.ShapeDtypeStruct((1, ROWS), jnp.float32),
             jax.ShapeDtypeStruct((OUT_ROWS, WIDTH), jnp.float32),
         ),
-        in_specs=[pl.BlockSpec(memory_space=pl.ANY)] * 4,
+        in_specs=[pl.BlockSpec(memory_space=pltpu.HBM)] * 4,
         out_specs=(vmem, vmem),
         scratch_shapes=scratch,
-        compiler_params=pltpu.CompilerParams(collective_id=0, has_side_effects=True),
+        compiler_params=pltpu.CompilerParams(
+            collective_id=0, has_side_effects=True, vmem_limit_bytes=55040 * 1024
+        ),
     )(features, labels, weights, sampled)
 
 

time: 68 us -> 65.8 us (0.968)
  Pallas kernels: 64.6 us -> 62.5 us
    pallas_call x1, Pallas kernels: 64.6 us -> 62.5 us  [head(): pl.pallas_call(head_kernel, out_shape=(jax.ShapeDtypeStruct((1, ROWS), jn...]
    unnamed x2 -> x6, local copies, waits for them, and re-layouts: 2.59 us -> 2.47 us
where the time goes in v4:
time: 65.8 us; the launch traced here: 65.6 us
  Pallas kernels  62.5 us (95%)
  local copies, waits for them, and re-layouts  2.47 us (4%)
    pallas_call x1, Pallas kernels, head(): pl.pallas_call(head_kernel, out_shape=(jax.ShapeDtypeStruct((1, ROWS), jn...  62.5 us
    unnamed x6, local copies, waits for them, and re-layouts  2.47 us

profile of v4, /device:TPU:1, one launch (start us, length us, event | category | flops | bytes accessed | tf_op | source)
XLA Modules:
  0.0 65.6 jit_solution(5849000809422788464)
XLA Ops:
  0.6 0.0 copy-start
  0.6 0.7 %copy-done = s32[256]{0:T(256)S(1)} copy-done((s32[256]{0:T(256)S(1)}, s32[256]{0:T(256)}, u32[]{:S(2)}) %copy-start) | copy-done | bytes 1048
  1.3 0.0 copy-start.1
  1.3 0.7 copy-done.1
  2.0 62.5 %shard_map.59 = (f32[1,128]{1,0:T(1,128)S(1)}, f32[32,512]{1,0:T(8,128)S(1)}) custom-call(bf16[128,512]{1,0:T(8,128)(2,1)} %feat_ref.1, s32[1,128]{1,0:T(1,128)S(1)} %bitcast.2, f32[1024,512]{1,0:T(8,128)} %bank_ref.1, s32[256]{0:T(256)S(1)} %copy-done), custom_call_target="tpu_custom_call" | custom-call | tf_op jit(solution)/shard_map/pallas_call | solution.py:505
  64.5 0.5 copy.8
  65.0 0.6 copy.9
Async XLA Ops:
  0.6 0.7 %copy-start = (s32[256]{0:T(256)S(1)}, s32[256]{0:T(256)}, u32[]{:S(2)}) copy-start(s32[256]{0:T(256)} %sampled_ref.1) | copy-start | bytes 3076
  1.3 0.7 copy-start.1

commit v5 on v4

--- a/solution.py
+++ b/solution.py
@@ -468,6 +468,10 @@
 
 def head(features, labels, weights, sampled):
     vmem = pl.BlockSpec(memory_space=pltpu.VMEM)
+    operands = [
+        pltpu.with_memory_space_constraint(one, pltpu.HBM)
+        for one in (features, labels, weights, sampled)
+    ]
     dma = pltpu.SemaphoreType.DMA
     slots, column = NZ * NCORE, NYH * NYL
     scratch = [
@@ -512,9 +516,9 @@
         out_specs=(vmem, vmem),
         scratch_shapes=scratch,
         compiler_params=pltpu.CompilerParams(
-            collective_id=0, has_side_effects=True, vmem_limit_bytes=55040 * 1024
+            collective_id=0, has_side_effects=True, vmem_limit_bytes=48 * 1024 * 1024
         ),
-    )(features, labels, weights, sampled)
+    )(*operands)
 
 
 def per_device(features, labels, weights, sampled):

time: 65.8 us -> 64.5 us (0.980)
  local copies, waits for them, and re-layouts: 2.47 us -> 1.14 us
    unnamed x6 -> x2, local copies, waits for them, and re-layouts: 2.47 us -> 1.14 us
where the time goes in v5:
time: 64.5 us; the launch traced here: 64.3 us
  Pallas kernels  62.6 us (97%)
  local copies, waits for them, and re-layouts  1.14 us (2%)
    pallas_call x1, Pallas kernels, head(): pl.pallas_call(head_kernel, out_shape=(jax.ShapeDtypeStruct((1, ROWS), jn...  62.6 us

profile of v5, /device:TPU:1, one launch (start us, length us, event | category | flops | bytes accessed | tf_op | source)
XLA Modules:
  0.0 64.3 jit_solution(4957104828331221551)
XLA Ops:
  0.6 62.6 %shard_map.59 = (f32[1,128]{1,0:T(1,128)S(1)}, f32[32,512]{1,0:T(8,128)S(1)}) custom-call(bf16[128,512]{1,0:T(8,128)(2,1)} %feat_ref.1, s32[1,128]{1,0:T(1,128)} %bitcast.3, f32[1024,512]{1,0:T(8,128)} %bank_ref.1, s32[256]{0:T(256)} %sampled_ref.1), custom_call_target="tpu_custom_call" | custom-call | tf_op jit(solution)/shard_map/pallas_call | solution.py:509
  63.2 0.5 copy.8
  63.7 0.6 copy.9

commit v6 on v5

--- a/solution.py
+++ b/solution.py
@@ -239,6 +239,11 @@
         targets[2 * s] += target[:, :ROWS]
         targets[2 * s + 1] += target[:, ROWS:]
 
+    def forward_classes(h):
+        class_copies[0, 1, h].wait_recv()
+        for i in (2, 1, 3):
+            class_copies[i, 1, h].start()
+
     def receive_features(step):
         back = NZ - step
         for h in range(4):
@@ -252,10 +257,8 @@
                 if h % 2:
                     core_copies[step, h // 2].start()
                     core_copies[back, h // 2].start()
-            if step == 2 and h % 2:
-                class_copies[0, 1, h // 2].wait_recv()
-                for i in (2, 1, 3):
-                    class_copies[i, 1, h // 2].start()
+            if step == 3 and h == 1:
+                forward_classes(1)
         if step == NZ // 2:
             for h in (0, 2, 1, 3):
                 feat_copies[step, h].wait_recv()
@@ -274,6 +277,8 @@
 
     receive_features(1)
     receive_features(2)
+    forward_classes(0)
+    receive_features(3)
     receive_classes(0)
     for one in label_copies:
         one.wait_recv()
@@ -283,7 +288,6 @@
     def _(k):
         first_pass(lax.rem(k + (NZ - 1), NZ), 0)
 
-    receive_features(3)
     receive_cores(2, 6, 3, 5)
 
     @pl.loop(0, 4)

time: 64.5 us -> 63.6 us (0.986)
  Pallas kernels: 62.6 us -> 61.6 us
    pallas_call x1, Pallas kernels: 62.6 us -> 61.6 us  [head(): pl.pallas_call(head_kernel, out_shape=(jax.ShapeDtypeStruct((1, ROWS), jn...]
where the time goes in v6:
time: 63.6 us; the launch traced here: 63.4 us
  Pallas kernels  61.6 us (97%)
  local copies, waits for them, and re-layouts  1.14 us (2%)
  between operations  0.64 us (1%)
    pallas_call x1, Pallas kernels, head(): pl.pallas_call(head_kernel, out_shape=(jax.ShapeDtypeStruct((1, ROWS), jn...  61.6 us

profile of v6, /device:TPU:1, one launch (start us, length us, event | category | flops | bytes accessed | tf_op | source)
XLA Modules:
  0.0 63.4 jit_solution(14053834808951929017)
XLA Ops:
  0.6 61.6 %shard_map.59 = (f32[1,128]{1,0:T(1,128)S(1)}, f32[32,512]{1,0:T(8,128)S(1)}) custom-call(bf16[128,512]{1,0:T(8,128)(2,1)} %feat_ref.1, s32[1,128]{1,0:T(1,128)} %bitcast.3, f32[1024,512]{1,0:T(8,128)} %bank_ref.1, s32[256]{0:T(256)} %sampled_ref.1), custom_call_target="tpu_custom_call" | custom-call | tf_op jit(solution)/shard_map/pallas_call | solution.py:513
  62.3 0.5 copy.8
  62.8 0.6 copy.9

commit v7 on v6

--- a/solution.py
+++ b/solution.py
@@ -294,13 +294,12 @@
     def _(k):
         first_pass(2 + lax.div(k, 2) + lax.rem(k, 2) * (NZ - 4 - 2 * lax.div(k, 2)), 0)
 
+    receive_features(4)
     receive_classes(1)
 
     @pl.loop(0, 3)
     def _(k):
         first_pass(lax.rem(k + (NZ - 1), NZ), 1)
-
-    receive_features(4)
 
     @pl.loop(0, 4)
     def _(k):

time: 63.6 us -> 64 us (level)
  no operation moved by 1% of the time
where the time goes in v7:
time: 64 us; the launch traced here: 63.8 us
  Pallas kernels  62 us (97%)
  local copies, waits for them, and re-layouts  1.14 us (2%)
  between operations  0.64 us (1%)
    pallas_call x1, Pallas kernels, head(): pl.pallas_call(head_kernel, out_shape=(jax.ShapeDtypeStruct((1, ROWS), jn...  62 us

profile of v7, /device:TPU:1, one launch (start us, length us, event | category | flops | bytes accessed | tf_op | source)
XLA Modules:
  0.0 63.8 jit_solution(2073894403777050743)
XLA Ops:
  0.6 62.0 %shard_map.59 = (f32[1,128]{1,0:T(1,128)S(1)}, f32[32,512]{1,0:T(8,128)S(1)}) custom-call(bf16[128,512]{1,0:T(8,128)(2,1)} %feat_ref.1, s32[1,128]{1,0:T(1,128)} %bitcast.3, f32[1024,512]{1,0:T(8,128)} %bank_ref.1, s32[256]{0:T(256)} %sampled_ref.1), custom_call_target="tpu_custom_call" | custom-call | tf_op jit(solution)/shard_map/pallas_call | solution.py:512
  62.7 0.5 copy.8
  63.2 0.6 copy.9
